TPU v7x, 512 devices: a whole 4x8x8 slice. The times are simulated.
512 devices in a mesh: dp: 4 (over z_hi), ctx: 128 (over x, z_lo, y, core).
Axes of the slice: x: 4, y: 8, z: 8 (z_hi: 4, z_lo: 2; z = z_hi * 2 + z_lo), core: 2. Of those that a mesh axis runs over, the one named last changes fastest.
Arguments:
- values: bfloat16 [4, 16384, 512], P('dp', 'ctx'), may hold values from -6 to 6
- gates: bfloat16 [4, 16384, 512], P('dp', 'ctx'), may hold values from -6 to 6
- grad_out: bfloat16 [4, 16384, 512], P('dp', 'ctx'), may hold values from -6 to 6
- filters: float32 [512, 16384], P('ctx'), may hold values from -6 to 6
- skip: float32 [512], P('ctx'), may hold values from 0.5 to 1.5
Outputs:
- grad_values: bfloat16 [4, 16384, 512], P('dp', 'ctx')
- grad_gates: bfloat16 [4, 16384, 512], P('dp', 'ctx')
- grad_filters: float32 [512, 16384], P('ctx')
All inputs are finite; a program needn't handle non-finite values.
Results may differ from a plain program's by a relative error of at most 0.0049.
Values may be sent and summed in bfloat16 or wider, within the bound.
A program may use at most 64 MiB of HBM per device.

v0:
```python
import functools

import jax
import jax.numpy as jnp
import numpy as np
from jax import lax
from jax.experimental import pallas as pl
from jax.experimental.pallas import tpu as pltpu
from jax.sharding import PartitionSpec as P

MESH = pl.DeviceIdType.MESH
F32 = jnp.float32
BF16 = jnp.bfloat16


def split_table(table):
    table = np.asarray(table, np.float32)
    high = table.astype(jnp.bfloat16)
    low = (table - high.astype(np.float32)).astype(jnp.bfloat16)
    return high, low


def make_tables(n):
    line = np.arange(n, dtype=np.float64)
    turn = 2.0 * np.pi
    angle_one = turn * np.outer(line + 0.25, line) / n
    angle_mid = turn * np.outer(line + 0.25, line) / (n * n)
    angle_two = turn * (np.outer(line, line) % n) / n
    cos_one, sin_one = np.cos(angle_one), np.sin(angle_one)
    cos_two, sin_two = np.cos(angle_two), np.sin(angle_two)
    first_hi, first_lo = split_table(np.concatenate([cos_one, -sin_one], 0))
    first = np.concatenate([first_hi, first_lo], 1)
    fwd_hi, fwd_lo = split_table(np.block([[cos_two, -sin_two], [sin_two, cos_two]]))
    inv_hi, inv_lo = split_table(np.block([[cos_two, sin_two], [-sin_two, cos_two]]))
    last_hi, last_lo = split_table(np.concatenate([cos_one.T, -sin_one.T], 1))
    last = np.concatenate([last_hi, last_lo], 0)
    pick = np.zeros((256, 256), np.float32)
    for dest in range(32):
        for row in range(4):
            pick[8 * dest + row, 4 * dest + row] = 1.0
            pick[8 * dest + 4 + row, 128 + 4 * dest + row] = 1.0
    wide = np.stack([first, fwd_hi, fwd_lo, inv_hi, inv_lo, last, pick.astype(jnp.bfloat16)])
    eye = np.eye(n, dtype=np.float32).astype(jnp.bfloat16)
    mid = np.stack([np.cos(angle_mid), np.sin(angle_mid)]).astype(np.float32)
    return wide, eye, mid


def mm(a, b):
    return jnp.dot(a, b, preferred_element_type=F32)


def mm_t(a, b):
    return lax.dot_general(a, b, (((1,), (1,)), ((), ())), preferred_element_type=F32)


def split(x):
    high = x.astype(BF16)
    return high, (x - high.astype(F32)).astype(BF16)


def kernel(
    dims,
    vals_ref,
    gate_ref,
    grad_ref,
    filt_ref,
    skip_ref,
    wide_ref,
    eye_ref,
    mid_ref,
    gval_ref,
    ggate_ref,
    gfilt_ref,
    out_box,
    in_box,
    back_box,
    home_box,
    rows,
    hspec,
    spec,
    cross,
    parts,
    whole,
    sems,
):
    n, seqs, nx, nz, ny, nc = dims
    ctx = n
    chans = 4
    me = lax.axis_index("ctx")
    my_seq = lax.axis_index("dp")
    my_c = me % nc
    my_y = (me // nc) % ny
    my_z = (me // (nc * ny)) % nz
    my_x = me // (nc * ny * nz)

    def peer_of(step):
        c = (my_c + step % nc) % nc
        x = (my_x + (step // nc) % nx) % nx
        z = (my_z + (step // (nc * nx)) % nz) % nz
        y = (my_y + step // (nc * nx * nz)) % ny
        return ((x * nz + z) * ny + y) * nc + c

    barrier = pltpu.get_barrier_semaphore()

    def greet(step, carry):
        pl.semaphore_signal(
            barrier, inc=1, device_id=(my_seq, peer_of(step)), device_id_type=MESH
        )
        return carry

    lax.fori_loop(1, ctx, greet, 0)
    for other in range(1, seqs):
        pl.semaphore_signal(
            barrier, inc=1, device_id=((my_seq + other) % seqs, me), device_id_type=MESH
        )

    first, fwd_hi, fwd_lo = wide_ref[0], wide_ref[1], wide_ref[2]
    inv_hi, inv_lo, last, pick = wide_ref[3], wide_ref[4], wide_ref[5], wide_ref[6]
    cos_mid, sin_mid = mid_ref[0], mid_ref[1]

    for g in range(chans):
        cols = slice(128 * g, 128 * (g + 1))
        gated = (grad_ref[:, cols].astype(F32) * gate_ref[:, cols].astype(F32)).astype(BF16)
        both = jnp.concatenate([vals_ref[:, cols], gated], 1)
        out_box[32 * g : 32 * (g + 1)] = mm_t(pick, both).astype(BF16).reshape(32, 8, n)

    pl.semaphore_wait(barrier, ctx - 1 + seqs - 1)

    def exchange(src, dst, send_sem, recv_sem):
        def send(step, carry):
            peer = peer_of(step)
            pltpu.make_async_remote_copy(
                src_ref=src.at[peer],
                dst_ref=dst.at[me],
                send_sem=send_sem,
                recv_sem=recv_sem,
                device_id=(my_seq, peer),
                device_id_type=MESH,
            ).start()
            return carry

        lax.fori_loop(1, ctx, send, 0)
        pltpu.make_async_copy(src.at[me], dst.at[me], recv_sem).start()

    def drain(box, sem, count):
        part = box.at[pl.ds(0, count)]
        pltpu.make_async_copy(part, part, sem).wait()

    exchange(out_box, in_box, sems.at[0], sems.at[1])

    def forward(blocks, exact):
        count = len(blocks)
        data = jnp.concatenate(blocks, 1)
        if exact:
            data = data.astype(BF16)
            part = mm(first, jnp.concatenate([data, data], 0))
        else:
            high, low = split(data)
            part = mm(first, jnp.concatenate([high, high], 0)) + mm(first[:, :n], low)
        turned = []
        for i in range(count):
            re = part[:n, n * i : n * (i + 1)]
            im = part[n:, n * i : n * (i + 1)]
            turned.append(
                jnp.concatenate([re * cos_mid + im * sin_mid, im * cos_mid - re * sin_mid], 1)
            )
        high, low = split(jnp.concatenate(turned, 0))
        return mm(high, fwd_hi) + (mm(low, fwd_hi) + mm(high, fwd_lo))

    def inverse(re, im):
        high, low = split(jnp.concatenate([re, im], 1))
        part = mm(high, inv_hi) + (mm(low, inv_hi) + mm(high, inv_lo))
        res, ims = [], []
        for i in range(chans):
            re = part[n * i : n * (i + 1), :n]
            im = part[n * i : n * (i + 1), n:]
            res.append(re * cos_mid - im * sin_mid)
            ims.append(im * cos_mid + re * sin_mid)
        high, low = split(
            jnp.concatenate([jnp.concatenate(res, 1), jnp.concatenate(ims, 1)], 0)
        )
        both = mm(last, high)
        return both[:n] + (both[n:] + mm(last[:n], low))

    scale = float(n) ** -1
    unit = float(n) ** -2
    h = forward([filt_ref[pl.ds(c, n, stride=chans), :] for c in range(chans)], False)
    for c in range(chans):
        band = slice(n * c, n * (c + 1))
        hspec[band, :n] = (h[band, :n] * scale + skip_ref[c]) * unit
        hspec[band, n:] = h[band, n:] * (scale * unit)

    drain(in_box, sems.at[1], ctx)
    rows[...] = in_box[...].astype(F32).reshape(8 * n, n)
    spec[...] = forward([rows[pl.ds(c, n, stride=8), :] for c in range(8)], True)

    half = chans * n
    v_re, v_im = spec[:half, :n], spec[:half, n:]
    d_re, d_im = spec[half:, :n], spec[half:, n:]
    h_re, h_im = hspec[:, :n], hspec[:, n:]

    lag = inverse(d_re * v_re + d_im * v_im, d_im * v_re - d_re * v_im)
    lag = lag * (unit * (seqs**-0.5) * scale)
    for c in range(chans):
        cross[c] = lag[:, n * c : n * (c + 1)]
    for other in range(1, seqs):
        peer = (my_seq + other) % seqs
        pltpu.make_async_remote_copy(
            src_ref=cross.at[peer],
            dst_ref=parts.at[my_seq],
            send_sem=sems.at[4],
            recv_sem=sems.at[5],
            device_id=(peer, me),
            device_id_type=MESH,
        ).start()
    pltpu.make_async_copy(cross.at[my_seq], parts.at[my_seq], sems.at[5]).start()

    conv = inverse(h_re * v_re - h_im * v_im, h_re * v_im + h_im * v_re)
    gval = inverse(h_re * d_re + h_im * d_im, h_re * d_im - h_im * d_re)
    for c in range(chans):
        rows[pl.ds(c, n, stride=8), :] = conv[:, n * c : n * (c + 1)]
        rows[pl.ds(chans + c, n, stride=8), :] = gval[:, n * c : n * (c + 1)]
    back_box[...] = rows[...].reshape(n, 8, n).astype(BF16)
    exchange(back_box, home_box, sems.at[2], sems.at[3])

    drain(parts, sems.at[5], seqs)
    total = (parts[0] + parts[1]) + (parts[2] + parts[3])
    cross_sent = cross.at[pl.ds(0, seqs - 1)]
    pltpu.make_async_copy(cross_sent, cross_sent, sems.at[4]).wait()
    cross[0] = total
    for other in range(1, seqs):
        peer = (my_seq + other) % seqs
        pltpu.make_async_remote_copy(
            src_ref=cross.at[0],
            dst_ref=whole.at[my_seq],
            send_sem=sems.at[6],
            recv_sem=sems.at[7],
            device_id=(peer, me),
            device_id_type=MESH,
        ).start()
    pltpu.make_async_copy(cross.at[0], whole.at[my_seq], sems.at[7]).start()
    drain(whole, sems.at[7], seqs)
    for c in range(chans):
        gfilt_ref[pl.ds(c, n, stride=chans), :] = whole[c]

    drain(home_box, sems.at[3], ctx)
    for g in range(chans):
        cols = slice(128 * g, 128 * (g + 1))
        group = home_box[32 * g : 32 * (g + 1)].reshape(256, n)
        both = mm(mm_t(eye_ref[...], group).astype(BF16), pick)
        gval_ref[:, cols] = both[:, n:].astype(BF16)
        ggate_ref[:, cols] = (grad_ref[:, cols].astype(F32) * both[:, :n]).astype(BF16)

    drain(out_box, sems.at[0], ctx - 1)
    drain(back_box, sems.at[2], ctx - 1)
    drain(cross, sems.at[6], seqs - 1)


def per_device(sizes, values, gates, grad_out, filters, skip):
    seqs, ctx = sizes
    length = filters.shape[1]
    n = values.shape[1]
    chans = filters.shape[0]
    wide, eye, mid = (jnp.asarray(t) for t in make_tables(n))
    filt = filters.reshape(chans, n, n).transpose(1, 0, 2).reshape(n * chans, n)
    vmem = pl.BlockSpec(memory_space=pltpu.VMEM)
    smem = pl.BlockSpec(memory_space=pltpu.SMEM)
    gval, ggate, gfilt = pl.pallas_call(
        functools.partial(kernel, (n, seqs, 4, 2, 8, 2)),
        name="hyena_bwd",
        out_shape=(
            jax.ShapeDtypeStruct(values.shape[1:], BF16),
            jax.ShapeDtypeStruct(values.shape[1:], BF16),
            jax.ShapeDtypeStruct((n * chans, n), F32),
        ),
        in_specs=[vmem] * 4 + [smem] + [vmem] * 3,
        out_specs=(vmem,) * 3,
        scratch_shapes=[
            pltpu.VMEM((n, 8, n), BF16),
            pltpu.VMEM((n, 8, n), BF16),
            pltpu.VMEM((n, 8, n), BF16),
            pltpu.VMEM((n, 8, n), BF16),
            pltpu.VMEM((8 * n, n), F32),
            pltpu.VMEM((chans * n, 2 * n), F32),
            pltpu.VMEM((2 * chans * n, 2 * n), F32),
            pltpu.VMEM((chans, n, n), F32),
            pltpu.VMEM((seqs, n, n), F32),
            pltpu.VMEM((seqs, n, n), F32),
            pltpu.SemaphoreType.DMA((8,)),
        ],
        compiler_params=pltpu.CompilerParams(collective_id=0, has_side_effects=True),
    )(values[0], gates[0], grad_out[0], filt, skip, wide, eye, mid)
    gfilt = gfilt.reshape(n, chans, n).transpose(1, 0, 2).reshape(chans, length)
    return gval[None], ggate[None], gfilt


def solution(mesh):
    in_specs = (
        P("dp", "ctx", None),
        P("dp", "ctx", None),
        P("dp", "ctx", None),
        P("ctx", None),
        P("ctx"),
    )
    out_specs = (P("dp", "ctx", None), P("dp", "ctx", None), P("ctx", None))
    return jax.shard_map(
        functools.partial(per_device, (mesh.shape["dp"], mesh.shape["ctx"])),
        mesh=mesh,
        in_specs=in_specs,
        out_specs=out_specs,
        check_vma=False,
    )
```

profile of v0, /device:TPU:1, one launch (start us, length us, event | category | flops | bytes accessed | tf_op | source)
XLA Modules:
  0.0 57.9 jit_solution(9076015064748244067)
XLA Ops:
  0.6 54.2 %hyena_bwd.1 = (bf16[128,512]{1,0:T(8,128)(2,1)}, bf16[128,512]{1,0:T(8,128)(2,1)}, f32[512,128]{1,0:T(8,128)}) custom-call(bf16[128,512]{1,0:T(8,128)(2,1)} %bitcast.17, bf16[128,512]{1,0:T(8,128)(2,1)} %bitcast.18, bf16[128,512]{1,0:T(8,128)(2,1)} %bitcast.19, f32[512,128]{1,0:T(8,128)} %bitcast.15, f32[4]{0:T(128)} %skip_ref.1, ...), custom_call_target="tpu_custom_call" | custom-call | tf_op jit(solution)/shard_map/hyena_bwd/pallas_call | solution.py:268
  54.9 0.0 copy-start.1
  54.9 0.0 copy-start
  54.9 1.6 %copy.16 = bf16[1,128,512]{2,1,0:T(8,128)(2,1)} copy(bf16[1,128,512]{2,1,0:T(8,128)(2,1)} %bitcast.21) | data formatting | bytes 262144
  56.5 0.0 copy-done.1
  56.5 0.7 %copy.17 = bf16[1,128,512]{2,1,0:T(8,128)(2,1)} copy(bf16[1,128,512]{2,1,0:T(8,128)(2,1)S(1)} %bitcast.20) | data formatting | bytes 262144
  57.2 0.0 copy-done
  57.2 0.7 %copy.18 = f32[4,16384]{1,0:T(4,128)} copy(f32[4,16384]{1,0:T(4,128)S(1)} %bitcast.16) | data formatting | bytes 524288
Async XLA Ops:
  54.9 1.6 %copy-start.1 = (bf16[128,512]{1,0:T(8,128)(2,1)S(1)}, bf16[128,512]{1,0:T(8,128)(2,1)}, u32[]{:S(2)}) copy-start(bf16[128,512]{1,0:T(8,128)(2,1)} %get-tuple-element.7) | copy-start | bytes 393220
  54.9 2.3 %copy-start = (f32[512,128]{1,0:T(8,128)S(1)}, f32[512,128]{1,0:T(8,128)}, u32[]{:S(2)}) copy-start(f32[512,128]{1,0:T(8,128)} %get-tuple-element.8) | copy-start | bytes 786436
where the time goes:
time: 58 us; the launch traced here: 57.9 us
  Pallas kernels  54.2 us (93%)
  local copies, waits for them, and re-layouts  2.98 us (5%)
  between operations  0.66 us (1%)
    pallas_call x1, Pallas kernels, per_device(): pl.pallas_call(functools.partial(kernel, (n, seqs, 4, 2, 8, 2)), name='hy...  54.2 us
    unnamed x7, local copies, waits for them, and re-layouts  2.98 us

commit v1 on v0

--- a/solution.py
+++ b/solution.py
@@ -60,27 +60,33 @@
 
 def kernel(
     dims,
+    vals_hbm,
+    gate_hbm,
+    grad_hbm,
+    filt_hbm,
+    skip_hbm,
+    wide_hbm,
+    mid_hbm,
+    home_ref,
+    whole_ref,
     vals_ref,
     gate_ref,
     grad_ref,
     filt_ref,
     skip_ref,
     wide_ref,
-    eye_ref,
     mid_ref,
-    gval_ref,
-    ggate_ref,
-    gfilt_ref,
     out_box,
     in_box,
     back_box,
-    home_box,
     rows,
     hspec,
     spec,
+    own,
     cross,
     parts,
-    whole,
+    total,
+    load_sems,
     sems,
 ):
     n, seqs, nx, nz, ny, nc = dims
@@ -88,35 +94,61 @@
     chans = 4
     me = lax.axis_index("ctx")
     my_seq = lax.axis_index("dp")
-    my_c = me % nc
-    my_y = (me // nc) % ny
-    my_z = (me // (nc * ny)) % nz
+
+    loads = []
+    for i, (src, dst) in enumerate(
+        (
+            (grad_hbm, grad_ref),
+            (gate_hbm, gate_ref),
+            (vals_hbm, vals_ref),
+            (wide_hbm, wide_ref),
+            (filt_hbm, filt_ref),
+            (mid_hbm, mid_ref),
+            (skip_hbm, skip_ref),
+        )
+    ):
+        loads.append(pltpu.make_async_copy(src, dst, load_sems.at[i]))
+        loads[-1].start()
+
+    my_c = lax.rem(me, nc)
+    my_y = lax.rem(me // nc, ny)
+    my_z = lax.rem(me // (nc * ny), nz)
     my_x = me // (nc * ny * nz)
-
-    def peer_of(step):
-        c = (my_c + step % nc) % nc
-        x = (my_x + (step // nc) % nx) % nx
-        z = (my_z + (step // (nc * nx)) % nz) % nz
-        y = (my_y + step // (nc * nx * nz)) % ny
-        return ((x * nz + z) * ny + y) * nc + c
+    x_part = [lax.rem(my_x + d, nx) * (nz * ny * nc) for d in range(nx)]
+    z_part = [lax.rem(my_z + d, nz) * (ny * nc) for d in range(nz)]
+    c_part = [lax.rem(my_c + d, nc) for d in range(nc)]
+    lines = [x + z + c for x in x_part for z in z_part for c in c_part]
+
+    def each_peer(visit):
+        def plane(step, carry):
+            y = lax.rem(my_y + step, ny) * nc
+            for line in lines:
+                visit(line + y)
+            return carry
+
+        lax.fori_loop(ny // 2, ny, plane, 0)
+        lax.fori_loop(1, ny // 2, plane, 0)
+        for line in lines[1:]:
+            visit(line + my_y * nc)
 
     barrier = pltpu.get_barrier_semaphore()
 
-    def greet(step, carry):
+    def greet(peer):
         pl.semaphore_signal(
-            barrier, inc=1, device_id=(my_seq, peer_of(step)), device_id_type=MESH
+            barrier, inc=1, device_id=(my_seq, peer), device_id_type=MESH
         )
-        return carry
-
-    lax.fori_loop(1, ctx, greet, 0)
-    for other in range(1, seqs):
+
+    each_peer(greet)
+    others = [lax.rem(my_seq + d, seqs) for d in range(seqs)]
+    for d in range(1, seqs):
         pl.semaphore_signal(
-            barrier, inc=1, device_id=((my_seq + other) % seqs, me), device_id_type=MESH
+            barrier, inc=1, device_id=(others[d], me), device_id_type=MESH
         )
 
+    for load in loads[:4]:
+        load.wait()
     first, fwd_hi, fwd_lo = wide_ref[0], wide_ref[1], wide_ref[2]
     inv_hi, inv_lo, last, pick = wide_ref[3], wide_ref[4], wide_ref[5], wide_ref[6]
-    cos_mid, sin_mid = mid_ref[0], mid_ref[1]
 
     for g in range(chans):
         cols = slice(128 * g, 128 * (g + 1))
@@ -127,8 +159,7 @@
     pl.semaphore_wait(barrier, ctx - 1 + seqs - 1)
 
     def exchange(src, dst, send_sem, recv_sem):
-        def send(step, carry):
-            peer = peer_of(step)
+        def send(peer):
             pltpu.make_async_remote_copy(
                 src_ref=src.at[peer],
                 dst_ref=dst.at[me],
@@ -137,9 +168,8 @@
                 device_id=(my_seq, peer),
                 device_id_type=MESH,
             ).start()
-            return carry
-
-        lax.fori_loop(1, ctx, send, 0)
+
+        each_peer(send)
         pltpu.make_async_copy(src.at[me], dst.at[me], recv_sem).start()
 
     def drain(box, sem, count):
@@ -147,6 +177,10 @@
         pltpu.make_async_copy(part, part, sem).wait()
 
     exchange(out_box, in_box, sems.at[0], sems.at[1])
+
+    for load in loads[4:]:
+        load.wait()
+    cos_mid, sin_mid = mid_ref[0], mid_ref[1]
 
     def forward(blocks, exact):
         count = len(blocks)
@@ -202,18 +236,18 @@
     lag = inverse(d_re * v_re + d_im * v_im, d_im * v_re - d_re * v_im)
     lag = lag * (unit * (seqs**-0.5) * scale)
     for c in range(chans):
-        cross[c] = lag[:, n * c : n * (c + 1)]
-    for other in range(1, seqs):
-        peer = (my_seq + other) % seqs
+        own[c] = lag[:, n * c : n * (c + 1)]
+        cross[c] = lag[:, n * c : n * (c + 1)].astype(BF16)
+    far_first = sorted(range(1, seqs), key=lambda d: -min(d, seqs - d))
+    for d in far_first:
         pltpu.make_async_remote_copy(
-            src_ref=cross.at[peer],
-            dst_ref=parts.at[my_seq],
+            src_ref=cross.at[others[d]],
+            dst_ref=parts.at[d - 1],
             send_sem=sems.at[4],
             recv_sem=sems.at[5],
-            device_id=(peer, me),
+            device_id=(others[d], me),
             device_id_type=MESH,
         ).start()
-    pltpu.make_async_copy(cross.at[my_seq], parts.at[my_seq], sems.at[5]).start()
 
     conv = inverse(h_re * v_re - h_im * v_im, h_re * v_im + h_im * v_re)
     gval = inverse(h_re * d_re + h_im * d_im, h_re * d_im - h_im * d_re)
@@ -221,39 +255,51 @@
         rows[pl.ds(c, n, stride=8), :] = conv[:, n * c : n * (c + 1)]
         rows[pl.ds(chans + c, n, stride=8), :] = gval[:, n * c : n * (c + 1)]
     back_box[...] = rows[...].reshape(n, 8, n).astype(BF16)
-    exchange(back_box, home_box, sems.at[2], sems.at[3])
-
-    drain(parts, sems.at[5], seqs)
-    total = (parts[0] + parts[1]) + (parts[2] + parts[3])
-    cross_sent = cross.at[pl.ds(0, seqs - 1)]
-    pltpu.make_async_copy(cross_sent, cross_sent, sems.at[4]).wait()
-    cross[0] = total
-    for other in range(1, seqs):
-        peer = (my_seq + other) % seqs
+
+    @pl.when(my_seq < seqs // 2)
+    def _():
+        exchange(back_box, home_ref, sems.at[2], sems.at[3])
+
+    drain(parts, sems.at[5], seqs - 1)
+    summed = own[my_seq]
+    for d in range(seqs - 1):
+        summed = summed + parts[d].astype(F32)
+    total[0] = summed.astype(BF16)
+    for d in far_first:
         pltpu.make_async_remote_copy(
-            src_ref=cross.at[0],
-            dst_ref=whole.at[my_seq],
+            src_ref=total.at[0],
+            dst_ref=whole_ref.at[my_seq],
             send_sem=sems.at[6],
             recv_sem=sems.at[7],
-            device_id=(peer, me),
+            device_id=(others[d], me),
             device_id_type=MESH,
         ).start()
-    pltpu.make_async_copy(cross.at[0], whole.at[my_seq], sems.at[7]).start()
-    drain(whole, sems.at[7], seqs)
+    pltpu.make_async_copy(total.at[0], whole_ref.at[my_seq], sems.at[7]).start()
+
+    @pl.when(my_seq >= seqs // 2)
+    def _():
+        exchange(back_box, home_ref, sems.at[2], sems.at[3])
+
+    drain(out_box, sems.at[0], ctx - 1)
+    drain(cross, sems.at[4], seqs - 1)
+    drain(back_box, sems.at[2], ctx - 1)
+    drain(cross, sems.at[6], seqs - 1)
+    drain(home_ref, sems.at[3], ctx)
+    drain(whole_ref, sems.at[7], seqs)
+
+
+def finish(home_ref, whole_ref, grad_ref, pick_ref, eye_ref, gval_ref, ggate_ref, gfilt_ref):
+    n = grad_ref.shape[0]
+    chans = whole_ref.shape[0]
+    pick = pick_ref[...]
     for c in range(chans):
-        gfilt_ref[pl.ds(c, n, stride=chans), :] = whole[c]
-
-    drain(home_box, sems.at[3], ctx)
+        gfilt_ref[pl.ds(c, n, stride=chans), :] = whole_ref[c].astype(F32)
     for g in range(chans):
         cols = slice(128 * g, 128 * (g + 1))
-        group = home_box[32 * g : 32 * (g + 1)].reshape(256, n)
+        group = home_ref[32 * g : 32 * (g + 1)].reshape(256, n)
         both = mm(mm_t(eye_ref[...], group).astype(BF16), pick)
         gval_ref[:, cols] = both[:, n:].astype(BF16)
         ggate_ref[:, cols] = (grad_ref[:, cols].astype(F32) * both[:, :n]).astype(BF16)
-
-    drain(out_box, sems.at[0], ctx - 1)
-    drain(back_box, sems.at[2], ctx - 1)
-    drain(cross, sems.at[6], seqs - 1)
 
 
 def per_device(sizes, values, gates, grad_out, filters, skip):
@@ -262,21 +308,27 @@
     n = values.shape[1]
     chans = filters.shape[0]
     wide, eye, mid = (jnp.asarray(t) for t in make_tables(n))
+    pick = jnp.asarray(make_tables(n)[0][6])
     filt = filters.reshape(chans, n, n).transpose(1, 0, 2).reshape(n * chans, n)
     vmem = pl.BlockSpec(memory_space=pltpu.VMEM)
-    smem = pl.BlockSpec(memory_space=pltpu.SMEM)
-    gval, ggate, gfilt = pl.pallas_call(
+    anywhere = pl.BlockSpec(memory_space=pl.ANY)
+    home, whole = pl.pallas_call(
         functools.partial(kernel, (n, seqs, 4, 2, 8, 2)),
         name="hyena_bwd",
         out_shape=(
-            jax.ShapeDtypeStruct(values.shape[1:], BF16),
-            jax.ShapeDtypeStruct(values.shape[1:], BF16),
-            jax.ShapeDtypeStruct((n * chans, n), F32),
+            jax.ShapeDtypeStruct((n, 8, n), BF16),
+            jax.ShapeDtypeStruct((seqs, n, n), BF16),
         ),
-        in_specs=[vmem] * 4 + [smem] + [vmem] * 3,
-        out_specs=(vmem,) * 3,
+        in_specs=[anywhere] * 7,
+        out_specs=(anywhere,) * 2,
         scratch_shapes=[
-            pltpu.VMEM((n, 8, n), BF16),
+            pltpu.VMEM((n, chans * n), BF16),
+            pltpu.VMEM((n, chans * n), BF16),
+            pltpu.VMEM((n, chans * n), BF16),
+            pltpu.VMEM((n * chans, n), F32),
+            pltpu.SMEM((chans,), F32),
+            pltpu.VMEM(wide.shape, BF16),
+            pltpu.VMEM(mid.shape, F32),
             pltpu.VMEM((n, 8, n), BF16),
             pltpu.VMEM((n, 8, n), BF16),
             pltpu.VMEM((n, 8, n), BF16),
@@ -284,12 +336,25 @@
             pltpu.VMEM((chans * n, 2 * n), F32),
             pltpu.VMEM((2 * chans * n, 2 * n), F32),
             pltpu.VMEM((chans, n, n), F32),
-            pltpu.VMEM((seqs, n, n), F32),
-            pltpu.VMEM((seqs, n, n), F32),
+            pltpu.VMEM((chans, n, n), BF16),
+            pltpu.VMEM((seqs - 1, n, n), BF16),
+            pltpu.VMEM((1, n, n), BF16),
+            pltpu.SemaphoreType.DMA((7,)),
             pltpu.SemaphoreType.DMA((8,)),
         ],
         compiler_params=pltpu.CompilerParams(collective_id=0, has_side_effects=True),
-    )(values[0], gates[0], grad_out[0], filt, skip, wide, eye, mid)
+    )(values[0], gates[0], grad_out[0], filt, skip, wide, mid)
+    gval, ggate, gfilt = pl.pallas_call(
+        finish,
+        name="hyena_out",
+        out_shape=(
+            jax.ShapeDtypeStruct(values.shape[1:], BF16),
+            jax.ShapeDtypeStruct(values.shape[1:], BF16),
+            jax.ShapeDtypeStruct((n * chans, n), F32),
+        ),
+        in_specs=[vmem] * 5,
+        out_specs=(vmem,) * 3,
+    )(home, whole, grad_out[0], pick, eye)
     gfilt = gfilt.reshape(n, chans, n).transpose(1, 0, 2).reshape(chans, length)
     return gval[None], ggate[None], gfilt
 

time: 58 us -> 44.2 us (0.76)
  the two profiles are of different devices: /device:TPU:1 before, /device:TPU:4 now
where the time goes in v1:
time: 44.2 us; the launch traced here: 44 us
  Pallas kernels  43.4 us (98%)
  between operations  0.64 us (1%)
    pallas_call x1, Pallas kernels, per_device(): pl.pallas_call(functools.partial(kernel, (n, seqs, 4, 2, 8, 2)), name='hy...  41 us
    pallas_call x1, Pallas kernels, per_device(): pl.pallas_call(finish, name='hyena_out', out_shape=(jax.ShapeDtypeStruct(...  2.32 us

profile of v1, /device:TPU:4, one launch (start us, length us, event | category | flops | bytes accessed | tf_op | source)
XLA Modules:
  0.0 44.0 jit_solution(4753566856866361228)
XLA Ops:
  0.6 41.0 %hyena_bwd.1 = (bf16[128,8,128]{2,1,0:T(8,128)(2,1)}, bf16[4,128,128]{2,1,0:T(8,128)(2,1)}) custom-call(bf16[128,512]{1,0:T(8,128)(2,1)} %bitcast.18, bf16[128,512]{1,0:T(8,128)(2,1)} %bitcast.19, bf16[128,512]{1,0:T(8,128)(2,1)} %bitcast.15, f32[512,128]{1,0:T(8,128)} %bitcast.17, f32[4]{0:T(128)} %skip_hbm.1, bf16[7,256,256]{2,1,0:T(8,128)(2,1)} %constant.8.clone.wide_hbm, ...), custom_call_target="tpu_custom_call" | custom-call | tf_op jit(solution)/shard_map/hyena_bwd/pallas_call | solution.py:315
  41.7 2.3 %hyena_out.1 = (bf16[128,512]{1,0:T(8,128)(2,1)}, bf16[128,512]{1,0:T(8,128)(2,1)}, f32[512,128]{1,0:T(8,128)}) custom-call(bf16[128,8,128]{2,1,0:T(8,128)(2,1)} %get-tuple-element.8.home_ref, bf16[4,128,128]{2,1,0:T(8,128)(2,1)} %get-tuple-element.9.whole_ref, bf16[128,512]{1,0:T(8,128)(2,1)} %bitcast.16, bf16[256,256]{1,0:T(8,128)(2,1)} %constant.11.clone.pick_ref, ...), custom_call_target="tpu_custom_call" | custom-call | tf_op jit(solution)/shard_map/hyena_out/pallas_call | solution.py:347

commit v2 on v1

--- a/solution.py
+++ b/solution.py
@@ -88,6 +88,7 @@
     total,
     load_sems,
     sems,
+    ready,
 ):
     n, seqs, nx, nz, ny, nc = dims
     ctx = n
@@ -141,9 +142,12 @@
     each_peer(greet)
     others = [lax.rem(my_seq + d, seqs) for d in range(seqs)]
     for d in range(1, seqs):
-        pl.semaphore_signal(
-            barrier, inc=1, device_id=(others[d], me), device_id_type=MESH
-        )
+
+        @pl.when(my_seq + d < seqs)
+        def _(d=d):
+            pl.semaphore_signal(
+                barrier, inc=1, device_id=(others[d], me), device_id_type=MESH
+            )
 
     for load in loads[:4]:
         load.wait()
@@ -156,7 +160,7 @@
         both = jnp.concatenate([vals_ref[:, cols], gated], 1)
         out_box[32 * g : 32 * (g + 1)] = mm_t(pick, both).astype(BF16).reshape(32, 8, n)
 
-    pl.semaphore_wait(barrier, ctx - 1 + seqs - 1)
+    pl.semaphore_wait(barrier, ctx - 1 + my_seq)
 
     def exchange(src, dst, send_sem, recv_sem):
         def send(peer):
@@ -177,6 +181,13 @@
         pltpu.make_async_copy(part, part, sem).wait()
 
     exchange(out_box, in_box, sems.at[0], sems.at[1])
+    for d in range(1, seqs):
+
+        @pl.when(my_seq + d >= seqs)
+        def _(d=d):
+            pl.semaphore_signal(
+                ready, inc=1, device_id=(others[d], me), device_id_type=MESH
+            )
 
     for load in loads[4:]:
         load.wait()
@@ -229,16 +240,34 @@
     spec[...] = forward([rows[pl.ds(c, n, stride=8), :] for c in range(8)], True)
 
     half = chans * n
+
+    def send_back():
+        v_re, v_im = spec[:half, :n], spec[:half, n:]
+        d_re, d_im = spec[half:, :n], spec[half:, n:]
+        h_re, h_im = hspec[:, :n], hspec[:, n:]
+        conv = inverse(h_re * v_re - h_im * v_im, h_re * v_im + h_im * v_re)
+        gval = inverse(h_re * d_re + h_im * d_im, h_re * d_im - h_im * d_re)
+        for c in range(chans):
+            rows[pl.ds(c, n, stride=8), :] = conv[:, n * c : n * (c + 1)]
+            rows[pl.ds(chans + c, n, stride=8), :] = gval[:, n * c : n * (c + 1)]
+        back_box[...] = rows[...].reshape(n, 8, n).astype(BF16)
+        exchange(back_box, home_ref, sems.at[2], sems.at[3])
+
+    early = my_seq < seqs // 2
+
     v_re, v_im = spec[:half, :n], spec[:half, n:]
     d_re, d_im = spec[half:, :n], spec[half:, n:]
-    h_re, h_im = hspec[:, :n], hspec[:, n:]
-
     lag = inverse(d_re * v_re + d_im * v_im, d_im * v_re - d_re * v_im)
     lag = lag * (unit * (seqs**-0.5) * scale)
     for c in range(chans):
         own[c] = lag[:, n * c : n * (c + 1)]
         cross[c] = lag[:, n * c : n * (c + 1)].astype(BF16)
     far_first = sorted(range(1, seqs), key=lambda d: -min(d, seqs - d))
+
+    @pl.when(my_seq < seqs - 1)
+    def _():
+        pl.semaphore_wait(ready, seqs - 1 - my_seq)
+
     for d in far_first:
         pltpu.make_async_remote_copy(
             src_ref=cross.at[others[d]],
@@ -249,17 +278,7 @@
             device_id_type=MESH,
         ).start()
 
-    conv = inverse(h_re * v_re - h_im * v_im, h_re * v_im + h_im * v_re)
-    gval = inverse(h_re * d_re + h_im * d_im, h_re * d_im - h_im * d_re)
-    for c in range(chans):
-        rows[pl.ds(c, n, stride=8), :] = conv[:, n * c : n * (c + 1)]
-        rows[pl.ds(chans + c, n, stride=8), :] = gval[:, n * c : n * (c + 1)]
-    back_box[...] = rows[...].reshape(n, 8, n).astype(BF16)
-
-    @pl.when(my_seq < seqs // 2)
-    def _():
-        exchange(back_box, home_ref, sems.at[2], sems.at[3])
-
+    pl.when(early)(send_back)
     drain(parts, sems.at[5], seqs - 1)
     summed = own[my_seq]
     for d in range(seqs - 1):
@@ -276,9 +295,7 @@
         ).start()
     pltpu.make_async_copy(total.at[0], whole_ref.at[my_seq], sems.at[7]).start()
 
-    @pl.when(my_seq >= seqs // 2)
-    def _():
-        exchange(back_box, home_ref, sems.at[2], sems.at[3])
+    pl.when(jnp.logical_not(early))(send_back)
 
     drain(out_box, sems.at[0], ctx - 1)
     drain(cross, sems.at[4], seqs - 1)
@@ -312,14 +329,15 @@
     filt = filters.reshape(chans, n, n).transpose(1, 0, 2).reshape(n * chans, n)
     vmem = pl.BlockSpec(memory_space=pltpu.VMEM)
     anywhere = pl.BlockSpec(memory_space=pl.ANY)
+    in_hbm = pl.BlockSpec(memory_space=pltpu.HBM)
     home, whole = pl.pallas_call(
         functools.partial(kernel, (n, seqs, 4, 2, 8, 2)),
         name="hyena_bwd",
         out_shape=(
-            jax.ShapeDtypeStruct((n, 8, n), BF16),
-            jax.ShapeDtypeStruct((seqs, n, n), BF16),
+            pltpu.VMEM((n, 8, n), BF16),
+            pltpu.VMEM((seqs, n, n), BF16),
         ),
-        in_specs=[anywhere] * 7,
+        in_specs=[in_hbm] * 7,
         out_specs=(anywhere,) * 2,
         scratch_shapes=[
             pltpu.VMEM((n, chans * n), BF16),
@@ -341,8 +359,11 @@
             pltpu.VMEM((1, n, n), BF16),
             pltpu.SemaphoreType.DMA((7,)),
             pltpu.SemaphoreType.DMA((8,)),
+            pltpu.SemaphoreType.REGULAR,
         ],
-        compiler_params=pltpu.CompilerParams(collective_id=0, has_side_effects=True),
+        compiler_params=pltpu.CompilerParams(
+            collective_id=0, has_side_effects=True, vmem_limit_bytes=60 * 1024 * 1024
+        ),
     )(values[0], gates[0], grad_out[0], filt, skip, wide, mid)
     gval, ggate, gfilt = pl.pallas_call(
         finish,
@@ -354,6 +375,7 @@
         ),
         in_specs=[vmem] * 5,
         out_specs=(vmem,) * 3,
+        compiler_params=pltpu.CompilerParams(vmem_limit_bytes=8 << 20),
     )(home, whole, grad_out[0], pick, eye)
     gfilt = gfilt.reshape(n, chans, n).transpose(1, 0, 2).reshape(chans, length)
     return gval[None], ggate[None], gfilt

time: 44.2 us -> 40.3 us (0.912)
  the two profiles are of different devices: /device:TPU:4 before, /device:TPU:8 now
where the time goes in v2:
time: 40.3 us; the launch traced here: 40.2 us
  Pallas kernels  39.5 us (98%)
  between operations  0.69 us (2%)
    pallas_call x1, Pallas kernels, per_device(): pl.pallas_call(functools.partial(kernel, (n, seqs, 4, 2, 8, 2)), name='hy...  38.3 us
    pallas_call x1, Pallas kernels, per_device(): pl.pallas_call(finish, name='hyena_out', out_shape=(jax.ShapeDtypeStruct(...  1.2 us

profile of v2, /device:TPU:8, one launch (start us, length us, event | category | flops | bytes accessed | tf_op | source)
XLA Modules:
  0.0 40.2 jit_solution(18346999820234392498)
XLA Ops:
  0.6 0.0 copy-start
  0.6 0.0 copy-start.1
  0.7 0.0 copy-start.2
  0.7 38.3 %hyena_bwd.1 = (bf16[128,8,128]{2,1,0:T(8,128)(2,1)S(1)}, bf16[4,128,128]{2,1,0:T(8,128)(2,1)S(1)}) custom-call(bf16[128,512]{1,0:T(8,128)(2,1)} %bitcast.18, bf16[128,512]{1,0:T(8,128)(2,1)} %bitcast.19, bf16[128,512]{1,0:T(8,128)(2,1)} %bitcast.15, f32[512,128]{1,0:T(8,128)} %bitcast.17, f32[4]{0:T(128)} %skip_hbm.1, ...), custom_call_target="tpu_custom_call" | custom-call | tf_op jit(solution)/shard_map/hyena_bwd/pallas_call | solution.py:333
  39.0 0.0 copy-done
  39.0 0.0 copy-done.1
  39.0 0.0 copy-done.2
  39.0 1.2 %hyena_out.1 = (bf16[128,512]{1,0:T(8,128)(2,1)}, bf16[128,512]{1,0:T(8,128)(2,1)}, f32[512,128]{1,0:T(8,128)}) custom-call(bf16[128,8,128]{2,1,0:T(8,128)(2,1)S(1)} %get-tuple-element.8.home_ref, bf16[4,128,128]{2,1,0:T(8,128)(2,1)S(1)} %get-tuple-element.9.whole_ref, bf16[128,512]{1,0:T(8,128)(2,1)S(1)} %bitcast.16, bf16[256,256]{1,0:T(8,128)(2,1)S(1)} %copy-done.1, ...), custom_call_target="tpu_custom_call" | custom-call | tf_op jit(solution)/shard_map/hyena_out/pallas_call | solution.py:368
Async XLA Ops:
  0.6 38.3 %copy-start = (bf16[1,128,512]{2,1,0:T(8,128)(2,1)S(1)}, bf16[1,128,512]{2,1,0:T(8,128)(2,1)}, u32[]{:S(2)}) copy-start(bf16[1,128,512]{2,1,0:T(8,128)(2,1)} %param.11) | copy-start | bytes 393220
  0.6 38.3 %copy-start.1 = (bf16[256,256]{1,0:T(8,128)(2,1)S(1)}, bf16[256,256]{1,0:T(8,128)(2,1)}, u32[]{:S(2)}) copy-start(bf16[256,256]{1,0:T(8,128)(2,1)} %constant.11.clone.pick_ref) | copy-start | bytes 393220
  0.7 38.3 %copy-start.2 = (bf16[128,128]{1,0:T(8,128)(2,1)S(1)}, bf16[128,128]{1,0:T(8,128)(2,1)}, u32[]{:S(2)}) copy-start(bf16[128,128]{1,0:T(8,128)(2,1)} %constant.9.clone.eye_ref) | copy-start | bytes 98308

commit v3 on v2

--- a/solution.py
+++ b/solution.py
@@ -37,8 +37,9 @@
     pick = np.zeros((256, 256), np.float32)
     for dest in range(32):
         for row in range(4):
-            pick[8 * dest + row, 4 * dest + row] = 1.0
-            pick[8 * dest + 4 + row, 128 + 4 * dest + row] = 1.0
+            part, at = row // 2, row % 2
+            pick[128 * part + 4 * dest + at, 4 * dest + row] = 1.0
+            pick[128 * part + 4 * dest + 2 + at, 128 + 4 * dest + row] = 1.0
     wide = np.stack([first, fwd_hi, fwd_lo, inv_hi, inv_lo, last, pick.astype(jnp.bfloat16)])
     eye = np.eye(n, dtype=np.float32).astype(jnp.bfloat16)
     mid = np.stack([np.cos(angle_mid), np.sin(angle_mid)]).astype(np.float32)
@@ -88,6 +89,8 @@
     total,
     load_sems,
     sems,
+    arrived,
+    returned,
     ready,
 ):
     n, seqs, nx, nz, ny, nc = dims
@@ -158,7 +161,9 @@
         cols = slice(128 * g, 128 * (g + 1))
         gated = (grad_ref[:, cols].astype(F32) * gate_ref[:, cols].astype(F32)).astype(BF16)
         both = jnp.concatenate([vals_ref[:, cols], gated], 1)
-        out_box[32 * g : 32 * (g + 1)] = mm_t(pick, both).astype(BF16).reshape(32, 8, n)
+        mail = mm_t(pick, both).astype(BF16)
+        for part in range(2):
+            out_box[part, 32 * g : 32 * (g + 1)] = mail[n * part : n * (part + 1)].reshape(32, 4, n)
 
     pl.semaphore_wait(barrier, ctx - 1 + my_seq)
 
@@ -180,7 +185,8 @@
         part = box.at[pl.ds(0, count)]
         pltpu.make_async_copy(part, part, sem).wait()
 
-    exchange(out_box, in_box, sems.at[0], sems.at[1])
+    for part in range(2):
+        exchange(out_box.at[part], in_box.at[part], sems.at[part], arrived.at[part])
     for d in range(1, seqs):
 
         @pl.when(my_seq + d >= seqs)
@@ -216,7 +222,7 @@
         high, low = split(jnp.concatenate([re, im], 1))
         part = mm(high, inv_hi) + (mm(low, inv_hi) + mm(high, inv_lo))
         res, ims = [], []
-        for i in range(chans):
+        for i in range(part.shape[0] // n):
             re = part[n * i : n * (i + 1), :n]
             im = part[n * i : n * (i + 1), n:]
             res.append(re * cos_mid - im * sin_mid)
@@ -235,50 +241,74 @@
         hspec[band, :n] = (h[band, :n] * scale + skip_ref[c]) * unit
         hspec[band, n:] = h[band, n:] * (scale * unit)
 
-    drain(in_box, sems.at[1], ctx)
-    rows[...] = in_box[...].astype(F32).reshape(8 * n, n)
-    spec[...] = forward([rows[pl.ds(c, n, stride=8), :] for c in range(8)], True)
-
-    half = chans * n
-
-    def send_back():
-        v_re, v_im = spec[:half, :n], spec[:half, n:]
-        d_re, d_im = spec[half:, :n], spec[half:, n:]
-        h_re, h_im = hspec[:, :n], hspec[:, n:]
+    early = my_seq < seqs // 2
+    far_first = sorted(range(1, seqs), key=lambda d: -min(d, seqs - d))
+    pair = 2 * n
+
+    def send_parts(channels):
+        for d in far_first:
+
+            @pl.when(others[d] // 2 == channels)
+            def _(d=d):
+                pltpu.make_async_remote_copy(
+                    src_ref=cross.at[others[d]],
+                    dst_ref=parts.at[d - 1],
+                    send_sem=sems.at[4],
+                    recv_sem=sems.at[5],
+                    device_id=(others[d], me),
+                    device_id_type=MESH,
+                ).start()
+
+    def wait_ready():
+        @pl.when(my_seq < seqs - 1)
+        def _():
+            pl.semaphore_wait(ready, seqs - 1 - my_seq)
+
+    def send_back(part):
+        v_re, v_im = spec[part, :pair, :n], spec[part, :pair, n:]
+        d_re, d_im = spec[part, pair:, :n], spec[part, pair:, n:]
+        band = slice(pair * part, pair * (part + 1))
+        h_re, h_im = hspec[band, :n], hspec[band, n:]
         conv = inverse(h_re * v_re - h_im * v_im, h_re * v_im + h_im * v_re)
         gval = inverse(h_re * d_re + h_im * d_im, h_re * d_im - h_im * d_re)
-        for c in range(chans):
-            rows[pl.ds(c, n, stride=8), :] = conv[:, n * c : n * (c + 1)]
-            rows[pl.ds(chans + c, n, stride=8), :] = gval[:, n * c : n * (c + 1)]
-        back_box[...] = rows[...].reshape(n, 8, n).astype(BF16)
-        exchange(back_box, home_ref, sems.at[2], sems.at[3])
-
-    early = my_seq < seqs // 2
-
-    v_re, v_im = spec[:half, :n], spec[:half, n:]
-    d_re, d_im = spec[half:, :n], spec[half:, n:]
-    lag = inverse(d_re * v_re + d_im * v_im, d_im * v_re - d_re * v_im)
-    lag = lag * (unit * (seqs**-0.5) * scale)
-    for c in range(chans):
-        own[c] = lag[:, n * c : n * (c + 1)]
-        cross[c] = lag[:, n * c : n * (c + 1)].astype(BF16)
-    far_first = sorted(range(1, seqs), key=lambda d: -min(d, seqs - d))
-
-    @pl.when(my_seq < seqs - 1)
+        for c in range(2):
+            rows[pl.ds(c, n, stride=4), :] = conv[:, n * c : n * (c + 1)]
+            rows[pl.ds(2 + c, n, stride=4), :] = gval[:, n * c : n * (c + 1)]
+        back_box[part] = rows[...].reshape(n, 4, n).astype(BF16)
+        exchange(back_box.at[part], home_ref.at[part], sems.at[2 + part], returned.at[part])
+
+    for part in range(2):
+        pltpu.make_async_copy(in_box.at[part], in_box.at[part], arrived.at[part]).wait()
+        rows[...] = in_box[part].astype(F32).reshape(4 * n, n)
+        spec[part] = forward([rows[pl.ds(c, n, stride=4), :] for c in range(4)], True)
+        v_re, v_im = spec[part, :pair, :n], spec[part, :pair, n:]
+        d_re, d_im = spec[part, pair:, :n], spec[part, pair:, n:]
+        lag = inverse(d_re * v_re + d_im * v_im, d_im * v_re - d_re * v_im)
+        lag = lag * (unit * (seqs**-0.5) * scale)
+        for c in range(2):
+            own[2 * part + c] = lag[:, n * c : n * (c + 1)]
+            cross[2 * part + c] = lag[:, n * c : n * (c + 1)].astype(BF16)
+        if part == 0:
+
+            @pl.when(jnp.logical_not(early))
+            def _():
+                wait_ready()
+                send_parts(0)
+
+        else:
+
+            @pl.when(early)
+            def _():
+                wait_ready()
+                send_parts(0)
+
+            send_parts(1)
+
+    @pl.when(early)
     def _():
-        pl.semaphore_wait(ready, seqs - 1 - my_seq)
-
-    for d in far_first:
-        pltpu.make_async_remote_copy(
-            src_ref=cross.at[others[d]],
-            dst_ref=parts.at[d - 1],
-            send_sem=sems.at[4],
-            recv_sem=sems.at[5],
-            device_id=(others[d], me),
-            device_id_type=MESH,
-        ).start()
-
-    pl.when(early)(send_back)
+        for part in range(2):
+            send_back(part)
+
     drain(parts, sems.at[5], seqs - 1)
     summed = own[my_seq]
     for d in range(seqs - 1):
@@ -295,13 +325,18 @@
         ).start()
     pltpu.make_async_copy(total.at[0], whole_ref.at[my_seq], sems.at[7]).start()
 
-    pl.when(jnp.logical_not(early))(send_back)
-
-    drain(out_box, sems.at[0], ctx - 1)
+    @pl.when(jnp.logical_not(early))
+    def _():
+        for part in range(2):
+            send_back(part)
+
+    for part in range(2):
+        drain(out_box.at[part], sems.at[part], ctx - 1)
+        drain(back_box.at[part], sems.at[2 + part], ctx - 1)
     drain(cross, sems.at[4], seqs - 1)
-    drain(back_box, sems.at[2], ctx - 1)
     drain(cross, sems.at[6], seqs - 1)
-    drain(home_ref, sems.at[3], ctx)
+    for part in range(2):
+        drain(home_ref.at[part], returned.at[part], ctx)
     drain(whole_ref, sems.at[7], seqs)
 
 
@@ -313,7 +348,9 @@
         gfilt_ref[pl.ds(c, n, stride=chans), :] = whole_ref[c].astype(F32)
     for g in range(chans):
         cols = slice(128 * g, 128 * (g + 1))
-        group = home_ref[32 * g : 32 * (g + 1)].reshape(256, n)
+        group = jnp.concatenate(
+            [home_ref[part, 32 * g : 32 * (g + 1)].reshape(128, n) for part in range(2)], 0
+        )
         both = mm(mm_t(eye_ref[...], group).astype(BF16), pick)
         gval_ref[:, cols] = both[:, n:].astype(BF16)
         ggate_ref[:, cols] = (grad_ref[:, cols].astype(F32) * both[:, :n]).astype(BF16)
@@ -334,7 +371,7 @@
         functools.partial(kernel, (n, seqs, 4, 2, 8, 2)),
         name="hyena_bwd",
         out_shape=(
-            pltpu.VMEM((n, 8, n), BF16),
+            pltpu.VMEM((2, n, 4, n), BF16),
             pltpu.VMEM((seqs, n, n), BF16),
         ),
         in_specs=[in_hbm] * 7,
@@ -347,18 +384,20 @@
             pltpu.SMEM((chans,), F32),
             pltpu.VMEM(wide.shape, BF16),
             pltpu.VMEM(mid.shape, F32),
-            pltpu.VMEM((n, 8, n), BF16),
-            pltpu.VMEM((n, 8, n), BF16),
-            pltpu.VMEM((n, 8, n), BF16),
-            pltpu.VMEM((8 * n, n), F32),
+            pltpu.VMEM((2, n, 4, n), BF16),
+            pltpu.VMEM((2, n, 4, n), BF16),
+            pltpu.VMEM((2, n, 4, n), BF16),
+            pltpu.VMEM((4 * n, n), F32),
             pltpu.VMEM((chans * n, 2 * n), F32),
-            pltpu.VMEM((2 * chans * n, 2 * n), F32),
+            pltpu.VMEM((2, chans * n, 2 * n), F32),
             pltpu.VMEM((chans, n, n), F32),
             pltpu.VMEM((chans, n, n), BF16),
             pltpu.VMEM((seqs - 1, n, n), BF16),
             pltpu.VMEM((1, n, n), BF16),
             pltpu.SemaphoreType.DMA((7,)),
             pltpu.SemaphoreType.DMA((8,)),
+            pltpu.SemaphoreType.DMA((2,)),
+            pltpu.SemaphoreType.DMA((2,)),
             pltpu.SemaphoreType.REGULAR,
         ],
         compiler_params=pltpu.CompilerParams(

time: 40.3 us -> 39.3 us (0.975)
  the two profiles are of different devices: /device:TPU:8 before, /device:TPU:16 now
where the time goes in v3:
time: 39.3 us; the launch traced here: 39.2 us
  Pallas kernels  38.5 us (98%)
  between operations  0.69 us (2%)
    pallas_call x1, Pallas kernels, per_device(): pl.pallas_call(functools.partial(kernel, (n, seqs, 4, 2, 8, 2)), name='hy...  37.3 us
    pallas_call x1, Pallas kernels, per_device(): pl.pallas_call(finish, name='hyena_out', out_shape=(jax.ShapeDtypeStruct(...  1.21 us

profile of v3, /device:TPU:16, one launch (start us, length us, event | category | flops | bytes accessed | tf_op | source)
XLA Modules:
  0.0 39.2 jit_solution(15847382442912123882)
XLA Ops:
  0.6 0.0 copy-start
  0.6 0.0 copy-start.1
  0.7 0.0 copy-start.2
  0.7 37.3 %hyena_bwd.1 = (bf16[2,128,4,128]{3,2,1,0:T(4,128)(2,1)S(1)}, bf16[4,128,128]{2,1,0:T(8,128)(2,1)S(1)}) custom-call(bf16[128,512]{1,0:T(8,128)(2,1)} %bitcast.18, bf16[128,512]{1,0:T(8,128)(2,1)} %bitcast.19, bf16[128,512]{1,0:T(8,128)(2,1)} %bitcast.15, f32[512,128]{1,0:T(8,128)} %bitcast.17, f32[4]{0:T(128)} %skip_hbm.1, ...), custom_call_target="tpu_custom_call" | custom-call | tf_op jit(solution)/shard_map/hyena_bwd/pallas_call | solution.py:370
  38.0 0.0 copy-done
  38.0 0.0 copy-done.1
  38.0 0.0 copy-done.2
  38.0 1.2 %hyena_out.1 = (bf16[128,512]{1,0:T(8,128)(2,1)}, bf16[128,512]{1,0:T(8,128)(2,1)}, f32[512,128]{1,0:T(8,128)}) custom-call(bf16[2,128,4,128]{3,2,1,0:T(4,128)(2,1)S(1)} %get-tuple-element.8.home_ref, bf16[4,128,128]{2,1,0:T(8,128)(2,1)S(1)} %get-tuple-element.9.whole_ref, bf16[128,512]{1,0:T(8,128)(2,1)S(1)} %bitcast.16, bf16[256,256]{1,0:T(8,128)(2,1)S(1)} %copy-done.1, ...), custom_call_target="tpu_custom_call" | custom-call | tf_op jit(solution)/shard_map/hyena_out/pallas_call | solution.py:407
Async XLA Ops:
  0.6 37.3 %copy-start = (bf16[1,128,512]{2,1,0:T(8,128)(2,1)S(1)}, bf16[1,128,512]{2,1,0:T(8,128)(2,1)}, u32[]{:S(2)}) copy-start(bf16[1,128,512]{2,1,0:T(8,128)(2,1)} %param.11) | copy-start | bytes 393220
  0.6 37.3 %copy-start.1 = (bf16[256,256]{1,0:T(8,128)(2,1)S(1)}, bf16[256,256]{1,0:T(8,128)(2,1)}, u32[]{:S(2)}) copy-start(bf16[256,256]{1,0:T(8,128)(2,1)} %constant.11.clone.pick_ref) | copy-start | bytes 393220
  0.7 37.3 %copy-start.2 = (bf16[128,128]{1,0:T(8,128)(2,1)S(1)}, bf16[128,128]{1,0:T(8,128)(2,1)}, u32[]{:S(2)}) copy-start(bf16[128,128]{1,0:T(8,128)(2,1)} %constant.9.clone.eye_ref) | copy-start | bytes 98308

commit v4 on v3

--- a/solution.py
+++ b/solution.py
@@ -68,7 +68,9 @@
     skip_hbm,
     wide_hbm,
     mid_hbm,
-    home_ref,
+    eye_hbm,
+    gval_ref,
+    ggate_ref,
     whole_ref,
     vals_ref,
     gate_ref,
@@ -77,9 +79,11 @@
     skip_ref,
     wide_ref,
     mid_ref,
+    eye_ref,
     out_box,
     in_box,
     back_box,
+    home_ref,
     rows,
     hspec,
     spec,
@@ -109,6 +113,7 @@
             (filt_hbm, filt_ref),
             (mid_hbm, mid_ref),
             (skip_hbm, skip_ref),
+            (eye_hbm, eye_ref),
         )
     ):
         loads.append(pltpu.make_async_copy(src, dst, load_sems.at[i]))
@@ -121,18 +126,23 @@
     x_part = [lax.rem(my_x + d, nx) * (nz * ny * nc) for d in range(nx)]
     z_part = [lax.rem(my_z + d, nz) * (ny * nc) for d in range(nz)]
     c_part = [lax.rem(my_c + d, nc) for d in range(nc)]
-    lines = [x + z + c for x in x_part for z in z_part for c in c_part]
+    x_far = sorted(range(nx), key=lambda d: -min(d, nx - d))
+    lines = [x_part[d] + z + c for d in x_far for z in z_part[::-1] for c in c_part[::-1]]
 
     def each_peer(visit):
-        def plane(step, carry):
-            y = lax.rem(my_y + step, ny) * nc
+        def planes(step, carry):
+            up = lax.rem(my_y + (ny // 2 - step), ny) * nc
+            down = lax.rem(my_y + (ny // 2 + step), ny) * nc
             for line in lines:
-                visit(line + y)
+                visit(line + up)
+                visit(line + down)
             return carry
 
-        lax.fori_loop(ny // 2, ny, plane, 0)
-        lax.fori_loop(1, ny // 2, plane, 0)
-        for line in lines[1:]:
+        across = lax.rem(my_y + ny // 2, ny) * nc
+        for line in lines:
+            visit(line + across)
+        lax.fori_loop(1, ny // 2, planes, 0)
+        for line in lines[:-1]:
             visit(line + my_y * nc)
 
     barrier = pltpu.get_barrier_semaphore()
@@ -264,7 +274,7 @@
         def _():
             pl.semaphore_wait(ready, seqs - 1 - my_seq)
 
-    def send_back(part):
+    def results_of(part):
         v_re, v_im = spec[part, :pair, :n], spec[part, :pair, n:]
         d_re, d_im = spec[part, pair:, :n], spec[part, pair:, n:]
         band = slice(pair * part, pair * (part + 1))
@@ -275,6 +285,8 @@
             rows[pl.ds(c, n, stride=4), :] = conv[:, n * c : n * (c + 1)]
             rows[pl.ds(2 + c, n, stride=4), :] = gval[:, n * c : n * (c + 1)]
         back_box[part] = rows[...].reshape(n, 4, n).astype(BF16)
+
+    def send_back(part):
         exchange(back_box.at[part], home_ref.at[part], sems.at[2 + part], returned.at[part])
 
     for part in range(2):
@@ -304,9 +316,11 @@
 
             send_parts(1)
 
-    @pl.when(early)
-    def _():
-        for part in range(2):
+    for part in range(2):
+        results_of(part)
+
+        @pl.when(early)
+        def _(part=part):
             send_back(part)
 
     drain(parts, sems.at[5], seqs - 1)
@@ -337,15 +351,6 @@
     drain(cross, sems.at[6], seqs - 1)
     for part in range(2):
         drain(home_ref.at[part], returned.at[part], ctx)
-    drain(whole_ref, sems.at[7], seqs)
-
-
-def finish(home_ref, whole_ref, grad_ref, pick_ref, eye_ref, gval_ref, ggate_ref, gfilt_ref):
-    n = grad_ref.shape[0]
-    chans = whole_ref.shape[0]
-    pick = pick_ref[...]
-    for c in range(chans):
-        gfilt_ref[pl.ds(c, n, stride=chans), :] = whole_ref[c].astype(F32)
     for g in range(chans):
         cols = slice(128 * g, 128 * (g + 1))
         group = jnp.concatenate(
@@ -354,6 +359,23 @@
         both = mm(mm_t(eye_ref[...], group).astype(BF16), pick)
         gval_ref[:, cols] = both[:, n:].astype(BF16)
         ggate_ref[:, cols] = (grad_ref[:, cols].astype(F32) * both[:, :n]).astype(BF16)
+    drain(whole_ref, sems.at[7], seqs)
+
+
+def finish(gval_in, ggate_in, whole_ref, gval_hbm, ggate_hbm, gfilt_hbm, gfilt_ref, sems):
+    seqs, n = whole_ref.shape[:2]
+    copies = [
+        pltpu.make_async_copy(gval_in, gval_hbm, sems.at[0]),
+        pltpu.make_async_copy(ggate_in, ggate_hbm, sems.at[1]),
+        pltpu.make_async_copy(gfilt_ref, gfilt_hbm, sems.at[2]),
+    ]
+    copies[0].start()
+    copies[1].start()
+    for c in range(seqs):
+        gfilt_ref[pl.ds(c, n, stride=seqs), :] = whole_ref[c].astype(F32)
+    copies[2].start()
+    for copy in copies:
+        copy.wait()
 
 
 def per_device(sizes, values, gates, grad_out, filters, skip):
@@ -362,20 +384,20 @@
     n = values.shape[1]
     chans = filters.shape[0]
     wide, eye, mid = (jnp.asarray(t) for t in make_tables(n))
-    pick = jnp.asarray(make_tables(n)[0][6])
     filt = filters.reshape(chans, n, n).transpose(1, 0, 2).reshape(n * chans, n)
     vmem = pl.BlockSpec(memory_space=pltpu.VMEM)
     anywhere = pl.BlockSpec(memory_space=pl.ANY)
     in_hbm = pl.BlockSpec(memory_space=pltpu.HBM)
-    home, whole = pl.pallas_call(
+    gval, ggate, whole = pl.pallas_call(
         functools.partial(kernel, (n, seqs, 4, 2, 8, 2)),
         name="hyena_bwd",
         out_shape=(
-            pltpu.VMEM((2, n, 4, n), BF16),
+            pltpu.VMEM((n, chans * n), BF16),
+            pltpu.VMEM((n, chans * n), BF16),
             pltpu.VMEM((seqs, n, n), BF16),
         ),
-        in_specs=[in_hbm] * 7,
-        out_specs=(anywhere,) * 2,
+        in_specs=[in_hbm] * 8,
+        out_specs=(vmem, vmem, anywhere),
         scratch_shapes=[
             pltpu.VMEM((n, chans * n), BF16),
             pltpu.VMEM((n, chans * n), BF16),
@@ -384,6 +406,8 @@
             pltpu.SMEM((chans,), F32),
             pltpu.VMEM(wide.shape, BF16),
             pltpu.VMEM(mid.shape, F32),
+            pltpu.VMEM(eye.shape, BF16),
+            pltpu.VMEM((2, n, 4, n), BF16),
             pltpu.VMEM((2, n, 4, n), BF16),
             pltpu.VMEM((2, n, 4, n), BF16),
             pltpu.VMEM((2, n, 4, n), BF16),
@@ -394,7 +418,7 @@
             pltpu.VMEM((chans, n, n), BF16),
             pltpu.VMEM((seqs - 1, n, n), BF16),
             pltpu.VMEM((1, n, n), BF16),
-            pltpu.SemaphoreType.DMA((7,)),
+            pltpu.SemaphoreType.DMA((8,)),
             pltpu.SemaphoreType.DMA((8,)),
             pltpu.SemaphoreType.DMA((2,)),
             pltpu.SemaphoreType.DMA((2,)),
@@ -403,7 +427,7 @@
         compiler_params=pltpu.CompilerParams(
             collective_id=0, has_side_effects=True, vmem_limit_bytes=60 * 1024 * 1024
         ),
-    )(values[0], gates[0], grad_out[0], filt, skip, wide, mid)
+    )(values[0], gates[0], grad_out[0], filt, skip, wide, mid, eye)
     gval, ggate, gfilt = pl.pallas_call(
         finish,
         name="hyena_out",
@@ -412,10 +436,14 @@
             jax.ShapeDtypeStruct(values.shape[1:], BF16),
             jax.ShapeDtypeStruct((n * chans, n), F32),
         ),
-        in_specs=[vmem] * 5,
-        out_specs=(vmem,) * 3,
+        in_specs=[vmem] * 3,
+        out_specs=(in_hbm,) * 3,
+        scratch_shapes=[
+            pltpu.VMEM((n * chans, n), F32),
+            pltpu.SemaphoreType.DMA((3,)),
+        ],
         compiler_params=pltpu.CompilerParams(vmem_limit_bytes=8 << 20),
-    )(home, whole, grad_out[0], pick, eye)
+    )(gval, ggate, whole)
     gfilt = gfilt.reshape(n, chans, n).transpose(1, 0, 2).reshape(chans, length)
     return gval[None], ggate[None], gfilt
 

time: 39.3 us -> 37.7 us (0.959)
  the two profiles are of different devices: /device:TPU:16 before, /device:TPU:8 now
where the time goes in v4:
time: 37.7 us; the launch traced here: 37.6 us
  Pallas kernels  37 us (98%)
  between operations  0.64 us (2%)
    pallas_call x1, Pallas kernels, per_device(): pl.pallas_call(functools.partial(kernel, (n, seqs, 4, 2, 8, 2)), name='hy...  36.1 us
    pallas_call x1, Pallas kernels, per_device(): pl.pallas_call(finish, name='hyena_out', out_shape=(jax.ShapeDtypeStruct(...  0.82 us

profile of v4, /device:TPU:8, one launch (start us, length us, event | category | flops | bytes accessed | tf_op | source)
XLA Modules:
  0.0 37.6 jit_solution(14557173462543718716)
XLA Ops:
  0.6 36.1 %hyena_bwd.1 = (bf16[128,512]{1,0:T(8,128)(2,1)S(1)}, bf16[128,512]{1,0:T(8,128)(2,1)S(1)}, bf16[4,128,128]{2,1,0:T(8,128)(2,1)S(1)}) custom-call(bf16[128,512]{1,0:T(8,128)(2,1)} %bitcast.16, bf16[128,512]{1,0:T(8,128)(2,1)} %bitcast.17, bf16[128,512]{1,0:T(8,128)(2,1)} %bitcast.18, f32[512,128]{1,0:T(8,128)} %bitcast.15, f32[4]{0:T(128)} %skip_hbm.1, ...), custom_call_target="tpu_custom_call" | custom-call | tf_op jit(solution)/shard_map/hyena_bwd/pallas_call | solution.py:391
  36.8 0.8 %hyena_out.1 = (bf16[128,512]{1,0:T(8,128)(2,1)}, bf16[128,512]{1,0:T(8,128)(2,1)}, f32[512,128]{1,0:T(8,128)}) custom-call(bf16[128,512]{1,0:T(8,128)(2,1)S(1)} %get-tuple-element.9.gval_in, bf16[128,512]{1,0:T(8,128)(2,1)S(1)} %get-tuple-element.10.ggate_in, bf16[4,128,128]{2,1,0:T(8,128)(2,1)S(1)} %get-tuple-element.11.whole_ref), custom_call_target="tpu_custom_call" | custom-call | tf_op jit(solution)/shard_map/hyena_out/pallas_call | solution.py:431

commit v5 on v4

--- a/solution.py
+++ b/solution.py
@@ -319,8 +319,9 @@
     for part in range(2):
         results_of(part)
 
-        @pl.when(early)
-        def _(part=part):
+    @pl.when(early)
+    def _():
+        for part in range(2):
             send_back(part)
 
     drain(parts, sems.at[5], seqs - 1)

time: 37.7 us -> 37.7 us (level)
  no operation moved by 1% of the time
where the time goes in v5:
time: 37.7 us; the launch traced here: 37.5 us
  Pallas kernels  36.9 us (98%)
  between operations  0.64 us (2%)
    pallas_call x1, Pallas kernels, per_device(): pl.pallas_call(functools.partial(kernel, (n, seqs, 4, 2, 8, 2)), name='hy...  36 us
    pallas_call x1, Pallas kernels, per_device(): pl.pallas_call(finish, name='hyena_out', out_shape=(jax.ShapeDtypeStruct(...  0.82 us

profile of v5, /device:TPU:8, one launch (start us, length us, event | category | flops | bytes accessed | tf_op | source)
XLA Modules:
  0.0 37.5 jit_solution(7725340577207697645)
XLA Ops:
  0.6 36.0 %hyena_bwd.1 = (bf16[128,512]{1,0:T(8,128)(2,1)S(1)}, bf16[128,512]{1,0:T(8,128)(2,1)S(1)}, bf16[4,128,128]{2,1,0:T(8,128)(2,1)S(1)}) custom-call(bf16[128,512]{1,0:T(8,128)(2,1)} %bitcast.16, bf16[128,512]{1,0:T(8,128)(2,1)} %bitcast.17, bf16[128,512]{1,0:T(8,128)(2,1)} %bitcast.18, f32[512,128]{1,0:T(8,128)} %bitcast.15, f32[4]{0:T(128)} %skip_hbm.1, ...), custom_call_target="tpu_custom_call" | custom-call | tf_op jit(solution)/shard_map/hyena_bwd/pallas_call | solution.py:392
  36.7 0.8 %hyena_out.1 = (bf16[128,512]{1,0:T(8,128)(2,1)}, bf16[128,512]{1,0:T(8,128)(2,1)}, f32[512,128]{1,0:T(8,128)}) custom-call(bf16[128,512]{1,0:T(8,128)(2,1)S(1)} %get-tuple-element.9.gval_in, bf16[128,512]{1,0:T(8,128)(2,1)S(1)} %get-tuple-element.10.ggate_in, bf16[4,128,128]{2,1,0:T(8,128)(2,1)S(1)} %get-tuple-element.11.whole_ref), custom_call_target="tpu_custom_call" | custom-call | tf_op jit(solution)/shard_map/hyena_out/pallas_call | solution.py:432

commit v6 on v5

--- a/solution.py
+++ b/solution.py
@@ -127,7 +127,7 @@
     z_part = [lax.rem(my_z + d, nz) * (ny * nc) for d in range(nz)]
     c_part = [lax.rem(my_c + d, nc) for d in range(nc)]
     x_far = sorted(range(nx), key=lambda d: -min(d, nx - d))
-    lines = [x_part[d] + z + c for d in x_far for z in z_part[::-1] for c in c_part[::-1]]
+    lines = [x_part[d] + z + c for d in x_far for c in c_part[::-1] for z in z_part[::-1]]
 
     def each_peer(visit):
         def planes(step, carry):

time: 37.7 us -> 37.6 us (level)
  no operation moved by 1% of the time
where the time goes in v6:
time: 37.6 us; the launch traced here: 37.5 us
  Pallas kernels  36.9 us (98%)
  between operations  0.64 us (2%)
    pallas_call x1, Pallas kernels, per_device(): pl.pallas_call(functools.partial(kernel, (n, seqs, 4, 2, 8, 2)), name='hy...  36 us
    pallas_call x1, Pallas kernels, per_device(): pl.pallas_call(finish, name='hyena_out', out_shape=(jax.ShapeDtypeStruct(...  0.82 us

profile of v6, /device:TPU:8, one launch (start us, length us, event | category | flops | bytes accessed | tf_op | source)
XLA Modules:
  0.0 37.5 jit_solution(12382831929250772641)
XLA Ops:
  0.6 36.0 %hyena_bwd.1 = (bf16[128,512]{1,0:T(8,128)(2,1)S(1)}, bf16[128,512]{1,0:T(8,128)(2,1)S(1)}, bf16[4,128,128]{2,1,0:T(8,128)(2,1)S(1)}) custom-call(bf16[128,512]{1,0:T(8,128)(2,1)} %bitcast.16, bf16[128,512]{1,0:T(8,128)(2,1)} %bitcast.17, bf16[128,512]{1,0:T(8,128)(2,1)} %bitcast.18, f32[512,128]{1,0:T(8,128)} %bitcast.15, f32[4]{0:T(128)} %skip_hbm.1, ...), custom_call_target="tpu_custom_call" | custom-call | tf_op jit(solution)/shard_map/hyena_bwd/pallas_call | solution.py:392
  36.7 0.8 %hyena_out.1 = (bf16[128,512]{1,0:T(8,128)(2,1)}, bf16[128,512]{1,0:T(8,128)(2,1)}, f32[512,128]{1,0:T(8,128)}) custom-call(bf16[128,512]{1,0:T(8,128)(2,1)S(1)} %get-tuple-element.9.gval_in, bf16[128,512]{1,0:T(8,128)(2,1)S(1)} %get-tuple-element.10.ggate_in, bf16[4,128,128]{2,1,0:T(8,128)(2,1)S(1)} %get-tuple-element.11.whole_ref), custom_call_target="tpu_custom_call" | custom-call | tf_op jit(solution)/shard_map/hyena_out/pallas_call | solution.py:432
